TPU v7x, 256 devices: a whole 4x4x8 slice. The times are simulated.
256 devices in a mesh: req: 4 (over x), exp: 64 (over z, y, core).
Axes of the slice: x: 4, y: 4, z: 8, core: 2. Of those that a mesh axis runs over, the one named last changes fastest.
Arguments:
- hidden: bfloat16 [256, 32, 2048], P(('req', 'exp')), may hold values from -6 to 6
- queries: bfloat16 [256, 32, 3072], P(('req', 'exp'))
- new_latent: bfloat16 [256, 32, 576], P(('req', 'exp')), may hold values from -6 to 6
- pages: bfloat16 [2048, 128, 576], P(('req', 'exp'))
- page_table: int32 [256, 8], P(('req', 'exp')), may hold values from 0 to 7, each once within a row
- cache_len: int32 [256], P(('req', 'exp')), may hold values from 1 to 992, as said below
- parents: int32 [256, 32], P(('req', 'exp')), may hold values from 0 to 30, as said below
- accept_path: int32 [256, 32], P(('req', 'exp')), may hold values from 0 to 31, as said below
- accept_count: int32 [256], P(('req', 'exp')), may hold values from 1 to 32, as said below
- key_up: bfloat16 [16, 128, 512], replicated, may hold values from -0.5 to 0.5
- value_up: bfloat16 [16, 512, 128], replicated, may hold values from -0.25 to 0.25
- out_proj: bfloat16 [2048, 2048], P(None, 'req'), may hold values from -0.125 to 0.125
- norm_gain: bfloat16 [2048], replicated, may hold values from 0.5 to 1.5
- route_ids: int32 [4, 64, 32, 6], P(None, 'exp'), may hold values from 0 to 63, all different within a row; in each aligned block of 32 rows (0 to 31, 32 to 63, ..., all dimensions but the last counted through in order) at most 6 rows name the same one
- route_weights: float32 [4, 64, 32, 6], P(None, 'exp'), may hold values from 0.2 to 1.2
- w_gate: bfloat16 [64, 2048, 1408], P('exp', None, 'req'), may hold values from -0.125 to 0.125
- w_up: bfloat16 [64, 2048, 1408], P('exp', None, 'req'), may hold values from -0.125 to 0.125
- w_down: bfloat16 [64, 1408, 2048], P('exp', 'req'), may hold values from -0.15625 to 0.15625
Outputs:
- layer_out: bfloat16 [256, 32, 2048], P(('req', 'exp'))
- new_pages: bfloat16 [2048, 128, 576], P(('req', 'exp'))
Inputs may be any that keep to these rules, and one draw needn't show every extreme that they name: `route_ids`: in each request no expert is named by more than 6 tokens, a bound that some block reaches. `page_table`: each row is an order of the 8 pages of the request's pool. `cache_len`: some request holds the largest length. parents[q, 0] = 0; for t >= 1 the parent of t is below t; one request's tree is a single chain. `accept_path`: entry k for k < accept_count is the ancestor at depth k of the last accepted token, entry 0 the root; later entries are 0. `accept_count`: one more than the depth of the last accepted token.
All inputs are finite; a program needn't handle non-finite values.
Results may differ from a plain program's by a relative error of at most 0.023.
Values may be sent and summed in bfloat16 or wider, within the bound.
A program may use at most 128 MiB of HBM per device.

v0:
```python
import math
import jax
import jax.numpy as jnp
from jax import lax
from jax.sharding import PartitionSpec as P

TOP = 6
TREE = 32


def ancestry(parent_row):
    count = parent_row.shape[0]
    ident = jnp.eye(count, dtype=jnp.int32)
    linked = (parent_row[:, None] == jnp.arange(count, dtype=jnp.int32)[None, :]).astype(jnp.int32)
    reach = jnp.minimum(ident + linked, 1)
    for sweep in range(count.bit_length()):
        reach = jnp.minimum(jnp.dot(reach, reach), 1)
    return reach


def attend(query_row, page_pool, table_row, length, parent_row, fresh, key_up, value_up):
    count = query_row.shape[0]
    heads = key_up.shape[0]
    nope = key_up.shape[1]
    latent = key_up.shape[2]
    shaped = query_row.reshape(count, heads, -1)
    scale = 1.0 / math.sqrt(shaped.shape[2])
    q_nope = shaped[:, :, :nope]
    q_rope = shaped[:, :, nope:]
    q_latent = jnp.einsum(
        "thn,hnc->thc", q_nope, key_up, preferred_element_type=jnp.float32
    ).astype(jnp.bfloat16)
    q_full = jnp.concatenate([q_latent, q_rope], axis=2)
    cache_rows = jnp.take(page_pool, table_row, axis=0).reshape(-1, page_pool.shape[2])
    score_cache = (
        jnp.einsum("thc,kc->thk", q_full, cache_rows, preferred_element_type=jnp.float32) * scale
    )
    score_tree = (
        jnp.einsum("thc,jc->thj", q_full, fresh, preferred_element_type=jnp.float32) * scale
    )
    live = jnp.arange(cache_rows.shape[0], dtype=jnp.int32) < length
    score_cache = jnp.where(live[None, None, :], score_cache, -1e30)
    score_tree = jnp.where(ancestry(parent_row)[:, None, :] > 0, score_tree, -1e30)
    peak = jnp.maximum(jnp.max(score_cache, axis=2), jnp.max(score_tree, axis=2))[:, :, None]
    exp_cache = jnp.exp(score_cache - peak)
    exp_tree = jnp.exp(score_tree - peak)
    total = jnp.sum(exp_cache, axis=2, keepdims=True) + jnp.sum(exp_tree, axis=2, keepdims=True)
    prob_cache = (exp_cache / total).astype(jnp.bfloat16)
    prob_tree = (exp_tree / total).astype(jnp.bfloat16)
    context = jnp.einsum(
        "thk,kc->thc", prob_cache, cache_rows[:, :latent], preferred_element_type=jnp.float32
    )
    context = context + jnp.einsum(
        "thj,jc->thc", prob_tree, fresh[:, :latent], preferred_element_type=jnp.float32
    )
    context = context.astype(jnp.bfloat16)
    head_out = jnp.einsum(
        "thc,hcv->thv", context, value_up, preferred_element_type=jnp.float32
    ).astype(jnp.bfloat16)
    return head_out.reshape(count, -1)


def write_rows(page_pool, table_row, length, path_row, count, fresh):
    pool_len = page_pool.shape[0]
    page_size = page_pool.shape[1]
    pool_ids = jnp.arange(pool_len, dtype=jnp.int32)
    match = table_row[None, :] == pool_ids[:, None]
    logical = jnp.sum(jnp.where(match, pool_ids[None, :], 0), axis=1)
    position = logical[:, None] * page_size + jnp.arange(page_size, dtype=jnp.int32)[None, :]
    offset = position - length
    valid = (offset >= 0) & (offset < count)
    source = jnp.take(path_row, jnp.clip(offset, 0, path_row.shape[0] - 1))
    written = jnp.take(fresh, source, axis=0)
    return jnp.where(valid[:, :, None], written, page_pool)


def slot_tables(route_rows, weight_rows, experts, capacity):
    expert_ids = jnp.arange(experts, dtype=jnp.int32)
    hits = route_rows[:, :, :, None] == expert_ids
    chosen = jnp.sum(hits.astype(jnp.int32), axis=2)
    weight_by = jnp.sum(jnp.where(hits, weight_rows[:, :, :, None], 0.0), axis=2)
    before = jnp.cumsum(chosen, axis=1) - chosen
    chosen_t = jnp.transpose(chosen, (0, 2, 1))
    before_t = jnp.transpose(before, (0, 2, 1))
    weight_t = jnp.transpose(weight_by, (0, 2, 1))
    slot_ids = jnp.arange(capacity, dtype=jnp.int32)
    placed = (chosen_t[:, :, None, :] > 0) & (
        before_t[:, :, None, :] == slot_ids[None, None, :, None]
    )
    weighted = jnp.where(placed, weight_t[:, :, None, :], 0.0)
    return (placed.astype(jnp.bfloat16), weighted)


def local(
    hidden,
    queries,
    new_latent,
    pages,
    page_table,
    cache_len,
    parents,
    accept_path,
    accept_count,
    key_up,
    value_up,
    out_proj,
    norm_gain,
    route_ids,
    route_weights,
    w_gate,
    w_up,
    w_down,
):
    width = hidden.shape[2]
    head_out = attend(
        queries[0], pages, page_table[0], cache_len[0], parents[0], new_latent[0], key_up, value_up
    )
    column_block = jnp.dot(
        lax.all_gather(head_out, "req", axis=0, tiled=True),
        out_proj,
        preferred_element_type=jnp.float32,
    ).astype(jnp.bfloat16)
    projected = lax.all_to_all(column_block, "req", split_axis=0, concat_axis=1, tiled=True)
    mixed = (hidden[0].astype(jnp.float32) + projected.astype(jnp.float32)).astype(jnp.bfloat16)
    mixed_f = mixed.astype(jnp.float32)
    normed = (
        mixed_f
        * lax.rsqrt(jnp.mean(mixed_f * mixed_f, axis=1, keepdims=True) + 1e-06)
        * norm_gain.astype(jnp.float32)
    ).astype(jnp.bfloat16)
    experts = lax.axis_size("exp") * w_gate.shape[0]
    capacity = max(2, min(TREE, 2 * TREE * TOP // experts))
    gate_local = w_gate[0]
    up_local = w_up[0]
    down_local = w_down[0]
    copies = lax.all_gather(normed[None], "req", axis=0, tiled=True)
    placed, weighted = slot_tables(route_ids[:, 0], route_weights[:, 0], experts, capacity)
    outbound = jnp.einsum(
        "gxct,gtd->xgcd", placed, copies, preferred_element_type=jnp.float32
    ).astype(jnp.bfloat16)
    slot_block = lax.all_to_all(outbound, "exp", split_axis=0, concat_axis=0, tiled=True)
    flat = slot_block.reshape(-1, width)
    gate_val = jnp.dot(flat, gate_local, preferred_element_type=jnp.float32)
    up_val = jnp.dot(flat, up_local, preferred_element_type=jnp.float32)
    active = (jax.nn.silu(gate_val) * up_val).astype(jnp.bfloat16)
    returned = lax.all_to_all(
        jnp.dot(active, down_local, preferred_element_type=jnp.float32)
        .astype(jnp.bfloat16)
        .reshape(slot_block.shape),
        "exp",
        split_axis=0,
        concat_axis=0,
        tiled=True,
    )
    partial_value = jnp.einsum("gxct,xgcd->gtd", weighted, returned.astype(jnp.float32))
    moe = lax.psum_scatter(
        partial_value.astype(jnp.bfloat16), "req", scatter_dimension=0, tiled=True
    ).astype(jnp.float32)[0]
    layer_out = (mixed_f + moe).astype(jnp.bfloat16)[None]
    new_pool = write_rows(
        pages, page_table[0], cache_len[0], accept_path[0], accept_count[0], new_latent[0]
    )
    return (layer_out, new_pool)


def solution(mesh):
    in_specs = (
        P(("req", "exp"), None, None),
        P(("req", "exp"), None, None),
        P(("req", "exp"), None, None),
        P(("req", "exp"), None, None),
        P(("req", "exp"), None),
        P(("req", "exp")),
        P(("req", "exp"), None),
        P(("req", "exp"), None),
        P(("req", "exp")),
        P(),
        P(),
        P(None, "req"),
        P(),
        P(None, "exp", None, None),
        P(None, "exp", None, None),
        P("exp", None, "req"),
        P("exp", None, "req"),
        P("exp", "req", None),
    )
    out_specs = (P(("req", "exp"), None, None), P(("req", "exp"), None, None))
    return jax.shard_map(local, mesh=mesh, in_specs=in_specs, out_specs=out_specs, check_vma=False)
```

profile of v0, /device:TPU:8, one launch (start us, length us, event | category | flops | bytes accessed | tf_op | source)
XLA Modules:
  0.0 495.9 jit_solution(1943214140383278034)
XLA Ops:
  7.2 0.0 copy-start
  7.2 1.4 reshape_squeeze.3
  8.6 0.7 slice.22
  9.3 0.7 fusion.78
  10.0 0.7 compare_and_fusion.1
  11.4 1.7 gather_fusion
  13.1 2.4 copy.166
  15.5 0.1 broadcast_bitcast_fusion
  15.6 0.4 fusion.18
  16.0 0.8 copy-done.6
  16.8 0.1 pad_maximum_fusion
  16.9 0.3 bitcast_select_fusion
  17.3 2.4 fusion.9
  19.7 0.1 copy.144
  19.7 0.4 convolution_minimum_fusion.4
  20.2 0.3 convolution_minimum_fusion.2
  20.5 0.3 fusion.23
  20.9 0.1 copy.143
  21.0 0.7 fusion.85
  21.7 0.1 copy.145
  21.8 2.1 fusion.10
  24.0 0.1 copy.146
  24.0 0.1 fusion.40
  24.1 0.1 copy.147
  24.2 2.1 divide_convert_fusion
  26.3 1.8 fusion.24
  28.1 2.5 fusion.22
  30.6 13.1 %all_gather.6 = bf16[128,2048]{1,0:T(8,128)(2,1)S(1)} all-gather(bf16[32,2048]{1,0:T(8,128)(2,1)S(1)} %bitcast.125), channel_id=1, replica_groups=mesh['req'=4,'exp'=64] {'req'}, dimensions={0}, use_global_device_ids=true | all-gather | bytes 655360 | tf_op jit(solution)/shard_map/all_gather | solution.py:119
  43.8 2.7 convolution_convert_fusion.2
  46.5 4.4 all-to-all-start
  50.9 0.2 convert_reduce_fusion
  51.1 0.1 reduce_window_sum.11
  51.2 5.6 %all-to-all-done = bf16[4,32,512]{2,1,0:T(8,128)(2,1)S(1)} async-done(((bf16[4,32,512]{2,1,0:T(8,128)(2,1)}), bf16[4,32,512]{2,1,0:T(8,128)(2,1)S(1)}, u32[]{:S(2)}, u32[]{:S(2)}) %all-to-all-start) | async-done | bytes 131104 | tf_op jit(solution)/shard_map/all_to_all | solution.py:123
  56.9 0.2 copy.151
  57.1 0.2 reshape.259
  57.4 0.1 multiply_reduce_fusion
  57.5 0.1 fusion.38
  57.6 13.7 %all_gather.7 = bf16[4,32,2048]{2,1,0:T(8,128)(2,1)S(1)} all-gather(bf16[1,32,2048]{2,1,0:T(8,128)(2,1)S(1)} %fusion.38), channel_id=1, replica_groups=mesh['req'=4,'exp'=64] {'req'}, dimensions={0}, use_global_device_ids=true | all-gather | bytes 655360 | tf_op jit(solution)/shard_map/all_gather | solution.py:136
  71.3 4.5 convert_bitcast_fusion
  75.8 10.3 %copy.157 = bf16[64,4,6,2048]{3,1,2,0:T(4,128)(2,1)} copy(bf16[64,4,6,2048]{3,0,2,1:T(8,128)(2,1)} %convert_bitcast_fusion) | data formatting | bytes 12582912 | tf_op jit(solution)/shard_map/convert_element_type | solution.py:140
  86.1 153.4 %all_to_all.23 = bf16[64,4,6,2048]{3,1,2,0:T(4,128)(2,1)S(1)} all-to-all(bf16[64,4,6,2048]{3,1,2,0:T(4,128)(2,1)} %copy.157), channel_id=1, replica_groups=mesh['req'=4,'exp'=64] {'exp'}, dimensions={0} | all-to-all | bytes 12582912 | tf_op jit(solution)/shard_map/all_to_all | solution.py:141
  239.5 10.7 %copy.158 = bf16[64,4,6,2048]{3,2,1,0:T(8,128)(2,1)} copy(bf16[64,4,6,2048]{3,1,2,0:T(4,128)(2,1)S(1)} %all_to_all.23) | data formatting | bytes 12582912 | tf_op jit(solution)/shard_map/all_to_all | solution.py:141
  250.2 11.1 %reshape.257 = bf16[1536,2048]{1,0:T(8,128)(2,1)} reshape(bf16[64,4,6,2048]{3,2,1,0:T(8,128)(2,1)} %copy.158) | data formatting | bytes 12582912 | tf_op jit(solution)/shard_map/reshape | solution.py:142
  261.3 7.0 %fusion.13 = f32[1536,352]{0,1:T(8,128)} fusion(bf16[1536,2048]{1,0:T(8,128)(2,1)} %reshape.257, bf16[1,2048,352]{1,2,0:T(8,128)(2,1)} %param.33), kind=kOutput, calls=%fused_computation.18 | convolution fusion | flops 2214592512 | bytes 9895936 | tf_op jit(solution)/shard_map/dot_general | solution.py:143
  268.3 12.2 %convolution_convert_fusion = bf16[1536,2048]{1,0:T(8,128)(2,1)} fusion(bf16[1,352,2048]{2,1,0:T(8,128)(2,1)} %param.35, bf16[1536,2048]{1,0:T(8,128)(2,1)} %reshape.257, f32[1536,352]{0,1:T(8,128)} %fusion.13, bf16[1,2048,352]{1,2,0:T(8,128)(2,1)} %param.34), kind=kOutput, calls=%fused_computation.3 | convolution fusion | flops 4435574784 | bytes 17629184 | tf_op jit(solution)/shard_map/dot_general | solution.py:147
  280.4 11.4 %reshape.258 = bf16[64,4,6,2048]{3,2,1,0:T(8,128)(2,1)} reshape(bf16[1536,2048]{1,0:T(8,128)(2,1)} %convolution_convert_fusion) | data formatting | bytes 12582912 | tf_op jit(solution)/shard_map/reshape | solution.py:149
  291.8 18.8 %copy.159 = bf16[64,4,6,2048]{3,1,2,0:T(4,128)(2,1)} copy(bf16[64,4,6,2048]{3,2,1,0:T(8,128)(2,1)} %reshape.258) | data formatting | bytes 12582912 | tf_op jit(solution)/shard_map/reshape | solution.py:149
  310.7 5.7 %all-to-all-start.2 = ((bf16[64,4,6,2048]{3,1,2,0:T(4,128)(2,1)}), bf16[64,4,6,2048]{3,1,2,0:T(4,128)(2,1)}, u32[]{:S(2)}, u32[]{:S(2)}) async-start(bf16[64,4,6,2048]{3,1,2,0:T(4,128)(2,1)} %copy.159), calls=%async_computation.2 | async-start | bytes 12582912 | tf_op jit(solution)/shard_map/all_to_all | solution.py:146
  316.4 0.0 reduce-scatter.2.cloned.1.call-start
  316.5 0.1 select_reduce_fusion.1
  316.6 0.3 select_reduce_fusion
  316.9 140.8 %all-to-all-done.2 = bf16[64,4,6,2048]{3,1,2,0:T(4,128)(2,1)} async-done(((bf16[64,4,6,2048]{3,1,2,0:T(4,128)(2,1)}), bf16[64,4,6,2048]{3,1,2,0:T(4,128)(2,1)}, u32[]{:S(2)}, u32[]{:S(2)}) %all-to-all-start.2) | async-done | bytes 6291488 | tf_op jit(solution)/shard_map/all_to_all | solution.py:146
  457.7 10.5 %fusion.6 = bf16[4,32,2048]{2,1,0:T(8,128)(2,1)} fusion(bf16[64,4,6,2048]{3,1,2,0:T(4,128)(2,1)} %all-to-all-done.2, bf16[4,64,32]{1,2,0:T(8,128)(2,1)S(1)} %bitcast.128, s32[4,64,32]{1,2,0:T(8,128)S(1)} %subtract_bitcast_fusion, pred[4,64,32]{1,2,0:T(8,128)(4,1)S(1)} %compare_bitcast_fusion), kind=kOutput, calls=%fused_computation.10 | convolution fusion | flops 201474048 | bytes 6873088 | tf_op jit(solution)/shard_map/gxct,xgcd->gtd/dot_general | solution.py:155
  468.2 0.0 reduce-scatter.2.cloned.1.call-update
  468.2 0.1 bitcast_clamp_fusion
  468.3 0.5 copy-done.2
  468.8 6.6 %gather_fusion.1 = s32[1024]{0:T(1024)S(1)} fusion(s32[32]{0:T(128)S(1)} %bitcast.120, s32[1024]{0:T(1024)S(1)} %bitcast_clamp_fusion), kind=kCustom, calls=%fused_computation.1 | custom fusion | bytes 12288 | tf_op jit(solution)/shard_map/jit(_take)/gather | solution.py:72
  475.4 0.1 fusion.68
  475.5 4.0 gather_fusion.2
  479.5 1.4 copy.161
  481.6 0.1 fusion.77
  481.7 2.6 select_select_fusion
  484.3 2.9 reduce-scatter.2.cloned.1.call-done
  487.2 1.7 fusion.39
  (49 shorter events, 0.3 us)
Async XLA Ops:
  7.2 8.4 %copy-start = (bf16[16,128,512]{2,1,0:T(8,128)(2,1)S(1)}, bf16[16,128,512]{2,1,0:T(8,128)(2,1)}, u32[]{:S(2)}) copy-start(bf16[16,128,512]{2,1,0:T(8,128)(2,1)} %param.27) | copy-start | bytes 6291460
  7.2 4.2 copy-start.4
  11.3 4.7 copy-start.9
  11.4 4.2 copy-start.11
  15.5 1.4 copy-start.5
  16.0 0.8 copy-start.6
  17.2 2.5 copy-start.15
  17.2 3.7 copy-start.3
  17.2 3.7 copy-start.7
  17.2 3.7 copy-start.10
  30.6 20.3 %copy-start.12 = (s32[4,1,32,6]{2,1,3,0:T(1,128)S(1)}, s32[4,1,32,6]{2,1,3,0:T(1,128)}, u32[]{:S(2)}) copy-start(s32[4,1,32,6]{2,1,3,0:T(1,128)} %param.31) | copy-start | bytes 9220
  30.6 20.6 %copy-start.14 = (bf16[2048]{0:T(1024)(128)(2,1)S(1)}, bf16[2048]{0:T(1024)(128)(2,1)}, u32[]{:S(2)}) copy-start(bf16[2048]{0:T(1024)(128)(2,1)} %param.30) | copy-start | bytes 12292
  46.5 10.9 %copy-start.8 = (bf16[1,32,2048]{2,1,0:T(8,128)(2,1)S(1)}, bf16[1,32,2048]{2,1,0:T(8,128)(2,1)}, u32[]{:S(2)}) copy-start(bf16[1,32,2048]{2,1,0:T(8,128)(2,1)} %param.18) | copy-start | bytes 393220
  46.5 10.4 %all-to-all-start = ((bf16[4,32,512]{2,1,0:T(8,128)(2,1)}), bf16[4,32,512]{2,1,0:T(8,128)(2,1)S(1)}, u32[]{:S(2)}, u32[]{:S(2)}) async-start(bf16[4,32,512]{2,1,0:T(8,128)(2,1)} %bitcast.14), calls=%async_computation | async-start | bytes 262144 | tf_op jit(solution)/shard_map/all_to_all | solution.py:123
  310.7 5.8 %copy-start.13 = (f32[4,1,32,6]{2,1,3,0:T(1,128)S(1)}, f32[4,1,32,6]{2,1,3,0:T(1,128)}, u32[]{:S(2)}) copy-start(f32[4,1,32,6]{2,1,3,0:T(1,128)} %param.32) | copy-start | bytes 9220
  310.7 5.8 %copy-start.16 = (s32[1,8]{1,0:T(1,128)S(1)}, s32[1,8]{1,0:T(1,128)}, u32[]{:S(2)}) copy-start(s32[1,8]{1,0:T(1,128)} %param.22) | copy-start | bytes 100
  310.7 147.0 %all-to-all-start.2 = ((bf16[64,4,6,2048]{3,1,2,0:T(4,128)(2,1)}), bf16[64,4,6,2048]{3,1,2,0:T(4,128)(2,1)}, u32[]{:S(2)}, u32[]{:S(2)}) async-start(bf16[64,4,6,2048]{3,1,2,0:T(4,128)(2,1)} %copy.159), calls=%async_computation.2 | async-start | bytes 12582912 | tf_op jit(solution)/shard_map/all_to_all | solution.py:146
  316.4 170.8 %reduce-scatter.2.cloned.1.call-start = ((), (), s32[]{:S(2)}) async-start(), calls=%async_computation.4 | async-start | bytes 655360 | tf_op jit(solution)/shard_map/reduce_scatter | solution.py:156
  468.2 0.7 copy-start.2
  481.7 7.2 %copy-start.1 = (bf16[16,128,512]{2,1,0:T(8,128)(2,1)S(1)}, bf16[16,128,512]{2,1,0:T(8,128)(2,1)}, u32[]{:S(2)}) copy-start(bf16[16,128,512]{2,1,0:T(8,128)(2,1)} %param.27) | copy-start | bytes 6291460
Sparse Core Ops, SparseCore 0:
  468.3 18.8 reduce-scatter.1
where the time goes:
time: 503 us; the launch traced here: 496 us
  blocking collectives  180 us (36%)
  waiting for transfers between devices  149 us (30%)
  local copies, waits for them, and re-layouts  82.8 us (16%)
  matrix products  45.8 us (9%)
  between operations  16 us (3%)
  other arithmetic  11.5 us (2%)
  starting transfers between devices  10.2 us (2%)
    all_to_all x1, blocking collectives, local(): lax.all_to_all(outbound, 'exp', split_axis=0, concat_axis=0, tiled=True)  153 us
    all_to_all x1, waiting for transfers between devices, local(): lax.all_to_all(jnp.dot(active, down_local, preferred_element_type=jnp.flo...  141 us
    reshape x2, local copies, waits for them, and re-layouts, local(): returned = lax.all_to_all(jnp.dot(active, down_local, preferred_element_t...  30.2 us
    all_gather x1, blocking collectives, local(): copies = lax.all_gather(normed[None], 'req', axis=0, tiled=True)  13.7 us
    all_gather x1, blocking collectives, local(): lax.all_gather(head_out, 'req', axis=0, tiled=True)  13.1 us
    dot_general x1, matrix products, local(): jnp.dot(active, down_local, preferred_element_type=jnp.float32)  12.2 us
    reshape x1, local copies, waits for them, and re-layouts, local(): flat = slot_block.reshape(-1, width)  11.1 us
    all_to_all x1, local copies, waits for them, and re-layouts, local(): lax.all_to_all(outbound, 'exp', split_axis=0, concat_axis=0, tiled=True)  10.7 us
  transfers between devices with their start and end apart: 3, of which 3 were waited for; matrix products, arithmetic and copies ran while one was open for 3% of the time, Pallas kernels for 0%

commit v1 on v0

--- a/solution.py
+++ b/solution.py
@@ -133,7 +133,14 @@
     gate_local = w_gate[0]
     up_local = w_up[0]
     down_local = w_down[0]
-    copies = lax.all_gather(normed[None], "req", axis=0, tiled=True)
+    x = normed[None]
+    peers = lax.axis_size("req")
+    current, tiles = (x, [x])
+    for _ in range(peers - 1):
+        current = lax.ppermute(current, "req", [(i, (i + 1) % peers) for i in range(peers)])
+        tiles.insert(0, current)
+    ravelled = jnp.concatenate(tiles, axis=0)
+    copies = jnp.roll(ravelled, (lax.axis_index("req") + 1) * x.shape[0], axis=0)
     placed, weighted = slot_tables(route_ids[:, 0], route_weights[:, 0], experts, capacity)
     outbound = jnp.einsum(
         "gxct,gtd->xgcd", placed, copies, preferred_element_type=jnp.float32

time: 503 us -> 521 us (1.036)
  waiting for transfers between devices: 149 us -> 176 us
  blocking collectives: 180 us -> 167 us
    ppermute x0 -> x3, waiting for transfers between devices: none -> 19.6 us  [local(): lax.ppermute(current, 'req', [(i, (i + 1) % peers) for i in range(peers)])]
    all_gather x1 -> x0, blocking collectives: 13.7 us -> none  [local(): copies = lax.all_gather(normed[None], 'req', axis=0, tiled=True)]
    reduce_scatter x1, waiting for transfers between devices: 2.91 us -> 9.24 us  [local(): lax.psum_scatter(partial_value.astype(jnp.bfloat16), 'req', scatter_dimen...]
  transfers between devices with their start and end apart: 3 -> 6, of which waited for: 3 -> 6; matrix products, arithmetic and copies ran while one was open for 3% -> 2% of each run, Pallas kernels for 0% -> 0%
where the time goes in v1:
time: 521 us; the launch traced here: 512 us
  waiting for transfers between devices  176 us (34%)
  blocking collectives  167 us (32%)
  local copies, waits for them, and re-layouts  81.7 us (16%)
  matrix products  45.5 us (9%)
  between operations  16 us (3%)
  other arithmetic  15.5 us (3%)
  starting transfers between devices  11 us (2%)
    all_to_all x1, blocking collectives, local(): lax.all_to_all(outbound, 'exp', split_axis=0, concat_axis=0, tiled=True)  153 us
    all_to_all x1, waiting for transfers between devices, local(): lax.all_to_all(jnp.dot(active, down_local, preferred_element_type=jnp.flo...  141 us
    reshape x2, local copies, waits for them, and re-layouts, local(): returned = lax.all_to_all(jnp.dot(active, down_local, preferred_element_t...  30.2 us
    ppermute x3, waiting for transfers between devices, local(): lax.ppermute(current, 'req', [(i, (i + 1) % peers) for i in range(peers)])  19.6 us
    all_gather x1, blocking collectives, local(): lax.all_gather(head_out, 'req', axis=0, tiled=True)  13.1 us
    dot_general x1, matrix products, local(): jnp.dot(active, down_local, preferred_element_type=jnp.float32)  12.2 us
    reshape x1, local copies, waits for them, and re-layouts, local(): flat = slot_block.reshape(-1, width)  11.1 us
    all_to_all x1, local copies, waits for them, and re-layouts, local(): lax.all_to_all(outbound, 'exp', split_axis=0, concat_axis=0, tiled=True)  10.7 us
  transfers between devices with their start and end apart: 6, of which 6 were waited for; matrix products, arithmetic and copies ran while one was open for 2% of the time, Pallas kernels for 0%

profile of v1, /device:TPU:8, one launch (start us, length us, event | category | flops | bytes accessed | tf_op | source)
XLA Modules:
  0.0 512.1 jit_solution(15684940632295591858)
XLA Ops:
  7.2 1.3 fusion.79
  8.5 1.2 compare_and_fusion.1
  9.7 1.2 reshape_squeeze.3
  11.7 0.8 select_reduce_fusion.1
  12.4 0.1 bitcast_clamp_fusion
  12.5 6.6 %gather_fusion.1 = s32[1024]{0:T(1024)S(1)} fusion(s32[32]{0:T(128)S(1)} %bitcast.120, s32[1024]{0:T(1024)S(1)} %bitcast_clamp_fusion), kind=kCustom, calls=%fused_computation.1 | custom fusion | bytes 12288 | tf_op jit(solution)/shard_map/jit(_take)/gather | solution.py:72
  19.1 0.7 fusion.69
  19.9 1.7 gather_fusion
  21.6 2.4 copy.166
  24.1 0.1 broadcast_bitcast_fusion
  24.2 1.6 bitcast_select_fusion
  25.8 0.4 fusion.18
  26.3 0.8 copy-done.5
  27.1 0.1 pad_maximum_fusion
  27.2 2.4 fusion.9
  29.6 0.1 copy.144
  29.7 0.4 convolution_minimum_fusion.4
  30.1 0.3 convolution_minimum_fusion.2
  30.4 0.3 fusion.23
  30.8 0.1 copy.143
  30.9 0.7 fusion.87
  31.7 0.1 copy.145
  31.7 2.1 fusion.10
  33.9 0.1 copy.146
  33.9 0.1 fusion.41
  34.0 0.1 copy.147
  34.1 2.2 divide_convert_fusion
  36.4 1.8 fusion.24
  38.1 2.5 fusion.22
  40.7 13.1 %all_gather.3 = bf16[128,2048]{1,0:T(8,128)(2,1)S(1)} all-gather(bf16[32,2048]{1,0:T(8,128)(2,1)S(1)} %bitcast.125), channel_id=1, replica_groups=mesh['req'=4,'exp'=64] {'req'}, dimensions={0}, use_global_device_ids=true | all-gather | bytes 655360 | tf_op jit(solution)/shard_map/all_gather | solution.py:119
  53.8 2.7 convolution_convert_fusion.2
  56.6 4.4 all-to-all-start
  61.0 6.0 %all-to-all-done = bf16[4,32,512]{2,1,0:T(8,128)(2,1)S(1)} async-done(((bf16[4,32,512]{2,1,0:T(8,128)(2,1)}), bf16[4,32,512]{2,1,0:T(8,128)(2,1)S(1)}, u32[]{:S(2)}, u32[]{:S(2)}) %all-to-all-start) | async-done | bytes 131104 | tf_op jit(solution)/shard_map/all_to_all | solution.py:123
  67.0 0.2 copy.151
  67.2 0.2 reshape.259
  67.4 0.1 multiply_reduce_fusion
  67.6 0.1 fusion.39
  67.7 0.6 collective-permute-start
  68.4 0.2 convert_reduce_fusion
  68.5 0.1 reduce_window_sum.11
  68.6 6.6 %collective-permute-done = bf16[1,32,2048]{2,1,0:T(8,128)(2,1)S(1)} collective-permute-done((bf16[1,32,2048]{2,1,0:T(8,128)(2,1)S(1)}, bf16[1,32,2048]{2,1,0:T(8,128)(2,1)S(1)}, u32[]{:S(2)}, u32[]{:S(2)}) %collective-permute-start) | collective-permute-done | bytes 131104 | tf_op jit(solution)/shard_map/ppermute | solution.py:140
  75.3 6.9 %collective-permute-done.1 = bf16[1,32,2048]{2,1,0:T(8,128)(2,1)S(1)} collective-permute-done((bf16[1,32,2048]{2,1,0:T(8,128)(2,1)S(1)}, bf16[1,32,2048]{2,1,0:T(8,128)(2,1)S(1)}, u32[]{:S(2)}, u32[]{:S(2)}) %collective-permute-start.1) | collective-permute-done | bytes 131104 | tf_op jit(solution)/shard_map/ppermute | solution.py:140
  82.1 0.2 collective-permute-start.2
  82.3 6.1 %collective-permute-done.2 = bf16[1,32,2048]{2,1,0:T(8,128)(2,1)S(1)} collective-permute-done((bf16[1,32,2048]{2,1,0:T(8,128)(2,1)S(1)}, bf16[1,32,2048]{2,1,0:T(8,128)(2,1)S(1)}, u32[]{:S(2)}, u32[]{:S(2)}) %collective-permute-start.2) | collective-permute-done | bytes 131104 | tf_op jit(solution)/shard_map/ppermute | solution.py:140
  88.6 4.5 convert_bitcast_fusion
  93.1 10.3 %copy.157 = bf16[64,4,6,2048]{3,1,2,0:T(4,128)(2,1)} copy(bf16[64,4,6,2048]{3,0,2,1:T(8,128)(2,1)} %convert_bitcast_fusion) | data formatting | bytes 12582912 | tf_op jit(solution)/shard_map/convert_element_type | solution.py:147
  103.4 153.4 %all_to_all.23 = bf16[64,4,6,2048]{3,1,2,0:T(4,128)(2,1)S(1)} all-to-all(bf16[64,4,6,2048]{3,1,2,0:T(4,128)(2,1)} %copy.157), channel_id=1, replica_groups=mesh['req'=4,'exp'=64] {'exp'}, dimensions={0} | all-to-all | bytes 12582912 | tf_op jit(solution)/shard_map/all_to_all | solution.py:148
  256.8 10.7 %copy.158 = bf16[64,4,6,2048]{3,2,1,0:T(8,128)(2,1)} copy(bf16[64,4,6,2048]{3,1,2,0:T(4,128)(2,1)S(1)} %all_to_all.23) | data formatting | bytes 12582912 | tf_op jit(solution)/shard_map/all_to_all | solution.py:148
  267.6 11.1 %reshape.257 = bf16[1536,2048]{1,0:T(8,128)(2,1)} reshape(bf16[64,4,6,2048]{3,2,1,0:T(8,128)(2,1)} %copy.158) | data formatting | bytes 12582912 | tf_op jit(solution)/shard_map/reshape | solution.py:149
  278.7 6.6 %fusion.13 = f32[1536,352]{0,1:T(8,128)} fusion(bf16[1536,2048]{1,0:T(8,128)(2,1)} %reshape.257, bf16[1,2048,352]{1,2,0:T(8,128)(2,1)S(1)} %copy-done.16), kind=kOutput, calls=%fused_computation.18 | convolution fusion | flops 2214592512 | bytes 9895936 | tf_op jit(solution)/shard_map/dot_general | solution.py:150
  285.3 12.2 %convolution_convert_fusion = bf16[1536,2048]{1,0:T(8,128)(2,1)} fusion(bf16[1,352,2048]{2,1,0:T(8,128)(2,1)} %param.35, bf16[1536,2048]{1,0:T(8,128)(2,1)} %reshape.257, f32[1536,352]{0,1:T(8,128)} %fusion.13, bf16[1,2048,352]{1,2,0:T(8,128)(2,1)} %param.34), kind=kOutput, calls=%fused_computation.3 | convolution fusion | flops 4435574784 | bytes 17629184 | tf_op jit(solution)/shard_map/dot_general | solution.py:154
  297.5 11.4 %reshape.258 = bf16[64,4,6,2048]{3,2,1,0:T(8,128)(2,1)} reshape(bf16[1536,2048]{1,0:T(8,128)(2,1)} %convolution_convert_fusion) | data formatting | bytes 12582912 | tf_op jit(solution)/shard_map/reshape | solution.py:156
  308.9 18.8 %copy.159 = bf16[64,4,6,2048]{3,1,2,0:T(4,128)(2,1)} copy(bf16[64,4,6,2048]{3,2,1,0:T(8,128)(2,1)} %reshape.258) | data formatting | bytes 12582912 | tf_op jit(solution)/shard_map/reshape | solution.py:156
  327.7 5.8 %all-to-all-start.2 = ((bf16[64,4,6,2048]{3,1,2,0:T(4,128)(2,1)}), bf16[64,4,6,2048]{3,1,2,0:T(4,128)(2,1)}, u32[]{:S(2)}, u32[]{:S(2)}) async-start(bf16[64,4,6,2048]{3,1,2,0:T(4,128)(2,1)} %copy.159), calls=%async_computation.2 | async-start | bytes 12582912 | tf_op jit(solution)/shard_map/all_to_all | solution.py:153
  333.5 0.0 reduce-scatter.2.cloned.1.call-start
  333.6 0.3 select_reduce_fusion
  333.8 140.9 %all-to-all-done.2 = bf16[64,4,6,2048]{3,1,2,0:T(4,128)(2,1)} async-done(((bf16[64,4,6,2048]{3,1,2,0:T(4,128)(2,1)}), bf16[64,4,6,2048]{3,1,2,0:T(4,128)(2,1)}, u32[]{:S(2)}, u32[]{:S(2)}) %all-to-all-start.2) | async-done | bytes 6291488 | tf_op jit(solution)/shard_map/all_to_all | solution.py:153
  474.7 10.5 %fusion.6 = bf16[4,32,2048]{2,1,0:T(8,128)(2,1)} fusion(bf16[64,4,6,2048]{3,1,2,0:T(4,128)(2,1)} %all-to-all-done.2, bf16[4,64,32]{1,2,0:T(8,128)(2,1)S(1)} %bitcast.128, s32[4,64,32]{1,2,0:T(8,128)S(1)} %subtract_bitcast_fusion, pred[4,64,32]{1,2,0:T(8,128)(4,1)S(1)} %compare_bitcast_fusion), kind=kOutput, calls=%fused_computation.10 | convolution fusion | flops 201474048 | bytes 6873088 | tf_op jit(solution)/shard_map/gxct,xgcd->gtd/dot_general | solution.py:162
  485.3 4.0 gather_fusion.2
  489.3 1.4 copy.161
  491.4 0.1 fusion.78
  491.5 2.6 select_select_fusion
  494.1 9.2 %reduce-scatter.2.cloned.1.call-done = bf16[1,32,2048]{2,1,0:T(8,128)(2,1)} async-done(((bf16[4,32,2048]{2,1,0:T(8,128)(2,1)}), bf16[1,32,2048]{2,1,0:T(8,128)(2,1)}) %reduce-scatter.2.cloned.1.call-update) | async-done | bytes 131088 | tf_op jit(solution)/shard_map/reduce_scatter | solution.py:163
  503.4 1.7 fusion.40
  (67 shorter events, 0.4 us)
Async XLA Ops:
  7.2 18.6 %copy-start = (bf16[16,128,512]{2,1,0:T(8,128)(2,1)S(1)}, bf16[16,128,512]{2,1,0:T(8,128)(2,1)}, u32[]{:S(2)}) copy-start(bf16[16,128,512]{2,1,0:T(8,128)(2,1)} %param.27) | copy-start | bytes 6291460
  7.2 5.3 %copy-start.2 = (s32[1,32]{1,0:T(1,128)S(1)}, s32[1,32]{1,0:T(1,128)}, u32[]{:S(2)}) copy-start(s32[1,32]{1,0:T(1,128)} %param.25) | copy-start | bytes 388
  11.0 8.1 %copy-start.10 = (bf16[32,16,192]{2,1,0:T(8,128)(2,1)}, bf16[32,16,192]{2,1,0:T(8,128)(2,1)S(1)}, u32[]{:S(2)}) copy-start(bf16[32,16,192]{2,1,0:T(8,128)(2,1)S(1)} %reshape_squeeze.3) | copy-start | bytes 589828
  12.5 7.3 %copy-start.4 = (bf16[8,128,576]{1,2,0:T(8,128)(2,1)S(1)}, bf16[8,128,576]{1,2,0:T(8,128)(2,1)}, u32[]{:S(2)}) copy-start(bf16[8,128,576]{1,2,0:T(8,128)(2,1)} %param.21) | copy-start | bytes 3538948
  19.9 4.2 copy-start.18
  19.9 4.2 slice-start.1
  21.6 4.2 slice-start
  24.2 2.1 copy-start.11
  25.8 3.8 copy-start.7
  26.3 0.8 copy-start.5
  27.1 2.5 copy-start.17
  27.1 3.7 copy-start.3
  27.2 3.7 copy-start.6
  27.2 3.7 copy-start.12
  33.9 2.5 copy-start.8
  40.6 20.4 %copy-start.15 = (bf16[2048]{0:T(1024)(128)(2,1)S(1)}, bf16[2048]{0:T(1024)(128)(2,1)}, u32[]{:S(2)}) copy-start(bf16[2048]{0:T(1024)(128)(2,1)} %param.30) | copy-start | bytes 12292
  53.8 13.6 %copy-start.9 = (bf16[1,32,2048]{2,1,0:T(8,128)(2,1)S(1)}, bf16[1,32,2048]{2,1,0:T(8,128)(2,1)}, u32[]{:S(2)}) copy-start(bf16[1,32,2048]{2,1,0:T(8,128)(2,1)} %param.18) | copy-start | bytes 393220
  56.6 11.8 %copy-start.13 = (s32[4,1,32,6]{2,1,3,0:T(1,128)S(1)}, s32[4,1,32,6]{2,1,3,0:T(1,128)}, u32[]{:S(2)}) copy-start(s32[4,1,32,6]{2,1,3,0:T(1,128)} %param.31) | copy-start | bytes 9220
  56.6 10.4 %all-to-all-start = ((bf16[4,32,512]{2,1,0:T(8,128)(2,1)}), bf16[4,32,512]{2,1,0:T(8,128)(2,1)S(1)}, u32[]{:S(2)}, u32[]{:S(2)}) async-start(bf16[4,32,512]{2,1,0:T(8,128)(2,1)} %bitcast.14), calls=%async_computation | async-start | bytes 262144 | tf_op jit(solution)/shard_map/all_to_all | solution.py:123
  67.7 7.6 %collective-permute-start = (bf16[1,32,2048]{2,1,0:T(8,128)(2,1)S(1)}, bf16[1,32,2048]{2,1,0:T(8,128)(2,1)S(1)}, u32[]{:S(2)}, u32[]{:S(2)}) collective-permute-start(bf16[1,32,2048]{2,1,0:T(8,128)(2,1)S(1)} %fusion.39), channel_id=1, source_target_pairs={{0,64},{64,128},{128,192},{192,0},{1,65},{65,129},{129,193},{193,1... | collective-permute-start | bytes 393224 | tf_op jit(solution)/shard_map/ppermute | solution.py:140
  75.3 6.9 %collective-permute-start.1 = (bf16[1,32,2048]{2,1,0:T(8,128)(2,1)S(1)}, bf16[1,32,2048]{2,1,0:T(8,128)(2,1)S(1)}, u32[]{:S(2)}, u32[]{:S(2)}) collective-permute-start(bf16[1,32,2048]{2,1,0:T(8,128)(2,1)S(1)} %collective-permute-done), channel_id=1, source_target_pairs={{0,64},{64,128},{128,192},{192,0},{1,65},{65,129},{129,193},{193,1... | collective-permute-start | bytes 393224 | tf_op jit(solution)/shard_map/ppermute | solution.py:140
  82.1 6.3 %collective-permute-start.2 = (bf16[1,32,2048]{2,1,0:T(8,128)(2,1)S(1)}, bf16[1,32,2048]{2,1,0:T(8,128)(2,1)S(1)}, u32[]{:S(2)}, u32[]{:S(2)}) collective-permute-start(bf16[1,32,2048]{2,1,0:T(8,128)(2,1)S(1)} %collective-permute-done.1), channel_id=1, source_target_pairs={{0,64},{64,128},{128,192},{192,0},{1,65},{65,129},{129,193},{193,1... | collective-permute-start | bytes 393224 | tf_op jit(solution)/shard_map/ppermute | solution.py:140
  267.6 11.1 %copy-start.16 = (bf16[1,2048,352]{1,2,0:T(8,128)(2,1)S(1)}, bf16[1,2048,352]{1,2,0:T(8,128)(2,1)}, u32[]{:S(2)}) copy-start(bf16[1,2048,352]{1,2,0:T(8,128)(2,1)} %param.33) | copy-start | bytes 4325380
  327.7 5.8 %copy-start.14 = (f32[4,1,32,6]{2,1,3,0:T(1,128)S(1)}, f32[4,1,32,6]{2,1,3,0:T(1,128)}, u32[]{:S(2)}) copy-start(f32[4,1,32,6]{2,1,3,0:T(1,128)} %param.32) | copy-start | bytes 9220
  327.7 147.0 %all-to-all-start.2 = ((bf16[64,4,6,2048]{3,1,2,0:T(4,128)(2,1)}), bf16[64,4,6,2048]{3,1,2,0:T(4,128)(2,1)}, u32[]{:S(2)}, u32[]{:S(2)}) async-start(bf16[64,4,6,2048]{3,1,2,0:T(4,128)(2,1)} %copy.159), calls=%async_computation.2 | async-start | bytes 12582912 | tf_op jit(solution)/shard_map/all_to_all | solution.py:153
  333.5 169.9 %reduce-scatter.2.cloned.1.call-start = ((), (), s32[]{:S(2)}) async-start(), calls=%async_computation.4 | async-start | bytes 655360 | tf_op jit(solution)/shard_map/reduce_scatter | solution.py:163
  491.5 13.5 %copy-start.1 = (bf16[16,128,512]{2,1,0:T(8,128)(2,1)S(1)}, bf16[16,128,512]{2,1,0:T(8,128)(2,1)}, u32[]{:S(2)}) copy-start(bf16[16,128,512]{2,1,0:T(8,128)(2,1)} %param.27) | copy-start | bytes 6291460
Sparse Core Ops, SparseCore 0:
  485.4 17.9 reduce-scatter.1
